TPU v7x, 256 devices: a whole 4x4x8 slice. The times are simulated.
256 devices in a mesh: blk: 32 (over z, y_lo, core), head: 8 (over x, y_hi).
Axes of the slice: x: 4, y: 4 (y_hi: 2, y_lo: 2; y = y_hi * 2 + y_lo), z: 8, core: 2. Of those that a mesh axis runs over, the one named last changes fastest.
Arguments:
- query: bfloat16 [32768, 4096], P(('blk', 'head')), may hold values from -6 to 6
- key: bfloat16 [32768, 1024], P(('blk', 'head')), may hold values from -6 to 6
- value: bfloat16 [32768, 1024], P(('blk', 'head')), may hold values from -6 to 6
- grad_out: bfloat16 [32768, 4096], P(('blk', 'head')), may hold values from -6 to 6
- doc_lengths: int32 [64], replicated, may hold values from 1 to 1024, 32768 in all
Outputs:
- attended: bfloat16 [32768, 4096], P(('blk', 'head'))
- grad_query: bfloat16 [32768, 4096], P(('blk', 'head'))
- grad_key: bfloat16 [32768, 1024], P(('blk', 'head'))
- grad_value: bfloat16 [32768, 1024], P(('blk', 'head'))
Inputs may be any that keep to these rules, and one draw needn't show every extreme that they name: `doc_lengths`: every document has at most 1024 tokens, one has exactly 1024, and the lengths sum to 32768.
All inputs are finite; a program needn't handle non-finite values.
Results may differ from a plain program's by a relative error of at most 0.0088.
Values may be sent and summed in bfloat16 or wider, within the bound.
No kernel may reach another device: no remote copies, remote signals or barrier semaphores. Data moves between devices by JAX's collectives and lax.ppermute only.
A program may use at most 128 MiB of HBM per device.

v0:
```python
import functools
import math

import jax
import jax.numpy as jnp
from jax import lax
from jax.experimental import pallas as pl
from jax.experimental.pallas import tpu as pltpu
from jax.sharding import PartitionSpec as P

HEAD_DIM = 128
SCALE = HEAD_DIM**-0.5
SCALE_LOG2 = SCALE * math.log2(math.e)
FLOOR = -1e30
TILE_Q = 128
TILE_K = 128
LAST_DIMS = (((1,), (1,)), ((), ()))


def passed_along(value, axis, steps):
    count = lax.axis_size(axis)
    initial, last = (max(0, -steps), min(count, count - steps))
    return lax.ppermute(value, axis, [(source, source + steps) for source in range(initial, last)])


def attention_kernel(
    heads, block, most, pad, counts_ref, start_ref, entered, earlier_ref, out_ref, earlier_out, own_out, window, sums
):
    stacked = heads * TILE_Q
    wide = 2 * heads * HEAD_DIM
    if pad:
        window[:pad] = jnp.zeros((pad, window.shape[1]), window.dtype)
    window[pad : pad + block] = earlier_ref[...]
    window[pad + block :] = entered[:, wide:]
    sums[...] = jnp.zeros_like(sums)

    def visit(count, tile):
        width = count * TILE_K
        first = block + (tile + 1) * TILE_Q - width
        span = pl.ds(pl.multiple_of(first + pad, 128), width)
        picked = pl.ds(pl.multiple_of(tile * TILE_Q, TILE_Q), TILE_Q)

        def stack(base):
            return jnp.concatenate(
                [entered[picked, base + h * HEAD_DIM : base + (h + 1) * HEAD_DIM] for h in range(heads)], axis=0
            )

        query = stack(0)
        grad = stack(heads * HEAD_DIM)
        keys = window[span, :HEAD_DIM]
        values = window[span, HEAD_DIM:]
        scores = lax.dot_general(query, keys, LAST_DIMS, preferred_element_type=jnp.float32)
        row = block + tile * TILE_Q + lax.broadcasted_iota(jnp.int32, (TILE_Q, width), 0)
        column = first + lax.broadcasted_iota(jnp.int32, (TILE_Q, width), 1)
        kept = (column <= row) & (column >= start_ref[picked, :])
        scores = jnp.where(kept[None], scores.reshape(heads, TILE_Q, width) * SCALE_LOG2, FLOOR)
        scores = scores.reshape(stacked, width)
        weights = jnp.exp2(scores - jnp.max(scores, axis=1, keepdims=True))
        inverse = 1.0 / jnp.sum(weights, axis=1, keepdims=True)
        weights_bf = weights.astype(jnp.bfloat16)
        out = (jnp.dot(weights_bf, values, preferred_element_type=jnp.float32) * inverse).astype(jnp.bfloat16)
        grad_wide = grad.astype(jnp.float32)
        delta = jnp.sum(grad_wide * out.astype(jnp.float32), axis=1, keepdims=True)
        grad_weights = lax.dot_general(grad, values, LAST_DIMS, preferred_element_type=jnp.float32)
        grad_scores = (weights * (grad_weights - delta)).astype(jnp.bfloat16)
        grad_query = jnp.dot(grad_scores, keys, preferred_element_type=jnp.float32) * (inverse * SCALE)
        grad_query = grad_query.astype(jnp.bfloat16)
        grad_scaled = (grad_wide * inverse).astype(jnp.bfloat16)
        query_scaled = (query.astype(jnp.float32) * (inverse * SCALE)).astype(jnp.bfloat16)
        sums[:HEAD_DIM, span] += jnp.dot(query_scaled.T, grad_scores, preferred_element_type=jnp.float32)
        sums[HEAD_DIM:, span] += jnp.dot(grad_scaled.T, weights_bf, preferred_element_type=jnp.float32)
        for h in range(heads):
            part = slice(h * TILE_Q, (h + 1) * TILE_Q)
            out_ref[picked, h * HEAD_DIM : (h + 1) * HEAD_DIM] = out[part]
            out_ref[picked, (heads + h) * HEAD_DIM : (heads + h + 1) * HEAD_DIM] = grad_query[part]

    @pl.loop(0, block // TILE_Q)
    def _(tile):
        needed = counts_ref[tile]
        for count in range(1, most + 1):
            pl.when(needed == count)(functools.partial(visit, count, tile))

    earlier_out[...] = sums[:, pad : pad + block].astype(jnp.bfloat16).T
    own_out[...] = sums[:, pad + block :].T


def attention(entered, earlier, starts):
    block, pair = earlier.shape
    heads = (entered.shape[1] - pair) // (2 * HEAD_DIM)
    most = -(-(TILE_Q + block - 1) // TILE_K)
    pad = max(0, most * TILE_K - block - TILE_Q)
    ends = block + TILE_Q * jnp.arange(1, block // TILE_Q + 1, dtype=jnp.int32)
    counts = jnp.clip((ends - starts[::TILE_Q] + TILE_K - 1) // TILE_K, 1, most).astype(jnp.int32)
    pairs = heads * block * block
    vmem = pl.BlockSpec(memory_space=pltpu.VMEM)
    return pl.pallas_call(
        functools.partial(attention_kernel, heads, block, most, pad),
        in_specs=[pl.BlockSpec(memory_space=pltpu.SMEM), vmem, vmem, vmem],
        out_specs=[vmem, vmem, vmem],
        scratch_shapes=[
            pltpu.VMEM((pad + 2 * block, pair), jnp.bfloat16),
            pltpu.VMEM((pair, pad + 2 * block), jnp.float32),
        ],
        out_shape=[
            jax.ShapeDtypeStruct(entered.shape, jnp.bfloat16),
            jax.ShapeDtypeStruct((block, pair), jnp.bfloat16),
            jax.ShapeDtypeStruct((block, pair), jnp.float32),
        ],
        compiler_params=pltpu.CompilerParams(vmem_limit_bytes=32 << 20),
        cost_estimate=pl.CostEstimate(
            flops=12 * pairs * HEAD_DIM, bytes_accessed=4 * entered.size, transcendentals=pairs
        ),
        name="attention",
    )(counts, starts[:, None], entered, earlier)


def moves(copies, sems):
    started = [pltpu.make_async_copy(source, target, sems.at[i]) for i, (source, target) in enumerate(copies)]
    for copy in started:
        copy.start()
    for copy in started:
        copy.wait()


def portions(count, wholes, joined):
    pairs, at = [], 0
    for whole in wholes:
        width = whole.shape[1] // count
        for h in range(count):
            pairs.append((whole.at[:, pl.ds(h * width, width)], joined.at[h, :, pl.ds(at, width)]))
        at += width
    return pairs


def pack_kernel(count, *refs):
    *wholes, joined, sems = refs
    moves(portions(count, wholes, joined), sems)


def unpack_kernel(count, joined, *refs):
    *wholes, sems = refs
    moves([(target, source) for source, target in portions(count, wholes, joined)], sems)


def pack(count, *wholes):
    rows = wholes[0].shape[0]
    width = sum(x.shape[1] for x in wholes) // count
    return pl.pallas_call(
        functools.partial(pack_kernel, count),
        in_specs=[pl.BlockSpec(memory_space=pl.ANY)] * len(wholes),
        out_specs=pl.BlockSpec(memory_space=pltpu.VMEM),
        out_shape=jax.ShapeDtypeStruct((count, rows, width), wholes[0].dtype),
        scratch_shapes=[pltpu.SemaphoreType.DMA((len(wholes) * count,))],
        name="pack",
    )(*wholes)


def unpack(joined, widths):
    count, rows, _ = joined.shape
    return pl.pallas_call(
        functools.partial(unpack_kernel, count),
        in_specs=[pl.BlockSpec(memory_space=pltpu.VMEM)],
        out_specs=[pl.BlockSpec(memory_space=pl.ANY)] * len(widths),
        out_shape=[jax.ShapeDtypeStruct((rows, count * width), joined.dtype) for width in widths],
        scratch_shapes=[pltpu.SemaphoreType.DMA((len(widths) * count,))],
        name="unpack",
    )(joined)


def exchange(value):
    return lax.all_to_all(value, "head", split_axis=0, concat_axis=0, tiled=True)


def per_device(query, key, value, grad_out, doc_lengths):
    rows = query.shape[0]
    count = lax.axis_size("head")
    block = rows * count
    pair = 2 * HEAD_DIM
    middle = query.shape[1] // count

    doc_ends = jnp.cumsum(doc_lengths)
    doc_starts = doc_ends - doc_lengths
    origin = lax.axis_index("blk") * block - block
    positions = origin + block + jnp.arange(block, dtype=jnp.int32)
    starts = jnp.max(jnp.where(doc_starts[None, :] <= positions[:, None], doc_starts[None, :], 0), axis=1)
    starts = (starts - origin).astype(jnp.int32)

    packed = pack(count, query, grad_out, key, value)
    entered = exchange(packed).reshape(block, -1)
    earlier = passed_along(entered[:, 2 * middle :], "blk", 1)
    out, earlier_sums, own_sums = attention(entered, earlier, starts)
    returned = passed_along(earlier_sums, "blk", -1)
    pair_sums = (own_sums + returned.astype(jnp.float32)).astype(jnp.bfloat16)
    out = lax.dynamic_update_slice(out, pair_sums, (0, 2 * middle))
    back = exchange(out.reshape(count, rows, -1))
    return tuple(unpack(back, (middle, middle, HEAD_DIM, HEAD_DIM)))


def solution(mesh):
    spec = P(("blk", "head"), None)
    return jax.shard_map(
        per_device,
        mesh=mesh,
        in_specs=(spec, spec, spec, spec, P()),
        out_specs=(spec, spec, spec, spec),
        check_vma=False,
    )
```

profile of v0, /device:TPU:192, one launch (start us, length us, event | category | flops | bytes accessed | tf_op | source)
XLA Modules:
  0.0 126.8 jit_solution(4978403415983566488)
XLA Ops:
  0.6 3.4 %pack.1 = bf16[8,128,1280]{2,1,0:T(8,128)(2,1)} custom-call(bf16[128,4096]{1,0:T(8,128)(2,1)} %refs_0_.1, bf16[128,4096]{1,0:T(8,128)(2,1)} %refs_1_.1, bf16[128,1024]{1,0:T(8,128)(2,1)} %refs_2_.1, bf16[128,1024]{1,0:T(8,128)(2,1)} %refs_3_.1), custom_call_target="tpu_custom_call" | custom-call | tf_op jit(solution)/shard_map/pack/pallas_call | solution.py:148
  4.1 0.0 copy-start
  4.1 6.9 %all-to-all-start = ((bf16[8,128,1280]{2,1,0:T(8,128)(2,1)}), bf16[8,128,1280]{2,1,0:T(8,128)(2,1)S(1)}, u32[]{:S(2)}, u32[]{:S(2)}) async-start(bf16[8,128,1280]{2,1,0:T(8,128)(2,1)} %pack.1), calls=%async_computation | async-start | bytes 5242880 | tf_op jit(solution)/shard_map/all_to_all | solution.py:171
  11.0 0.0 copy-done
  11.0 0.1 copy.12
  11.1 0.1 reduce-window.9
  11.2 0.1 reduce
  11.4 38.1 %all-to-all-done = bf16[8,128,1280]{2,1,0:T(8,128)(2,1)S(1)} async-done(((bf16[8,128,1280]{2,1,0:T(8,128)(2,1)}), bf16[8,128,1280]{2,1,0:T(8,128)(2,1)S(1)}, u32[]{:S(2)}, u32[]{:S(2)}) %all-to-all-start) | async-done | bytes 2621472 | tf_op jit(solution)/shard_map/all_to_all | solution.py:171
  49.5 0.8 slice.8
  50.3 1.9 %collective-permute-start = (bf16[1024,256]{1,0:T(8,128)(2,1)}, bf16[1024,256]{1,0:T(8,128)(2,1)}, u32[]{:S(2)}, u32[]{:S(2)}) collective-permute-start(bf16[1024,256]{1,0:T(8,128)(2,1)} %slice.8), channel_id=1, source_target_pairs={{0,8},{8,16},{16,24},{24,32},{32,40},{40,48},{48,56},{56,64},{64,7... | collective-permute-start | bytes 1572872 | tf_op jit(solution)/shard_map/ppermute | solution.py:23
  52.2 0.1 select_reduce_fusion
  52.4 0.1 slice.6
  52.4 0.2 copy.13.start_ref
  52.7 9.3 %collective-permute-done.earlier_ref = bf16[1024,256]{1,0:T(8,128)(2,1)} collective-permute-done((bf16[1024,256]{1,0:T(8,128)(2,1)}, bf16[1024,256]{1,0:T(8,128)(2,1)}, u32[]{:S(2)}, u32[]{:S(2)}) %collective-permute-start) | collective-permute-done | bytes 524320 | tf_op jit(solution)/shard_map/ppermute | solution.py:23
  62.0 14.9 %attention.1 = (bf16[1024,1280]{1,0:T(8,128)(2,1)S(1)}, bf16[1024,256]{1,0:T(8,128)(2,1)S(1)}, f32[1024,256]{1,0:T(8,128)S(1)}) custom-call(s32[8]{0:T(128)S(1)} %fusion.1.counts_ref, s32[1024,1]{1,0:T(8,128)S(1)} %copy.13.start_ref, bf16[1024,1280]{1,0:T(8,128)(2,1)S(1)} %bitcast.5, bf16[1024,256]{1,0:T(8,128)(2,1)} %collective-permute-done.earlier_ref), custom_call_target="tpu_custom_call" | custom-call | flops 6442450944 | bytes 5242880 | tf_op jit(solution)/shard_map/attention/pallas_call | solution.py:96
  76.9 1.9 %collective-permute-start.1 = (bf16[1024,256]{1,0:T(8,128)(2,1)S(1)}, bf16[1024,256]{1,0:T(8,128)(2,1)S(1)}, u32[]{:S(2)}, u32[]{:S(2)}) collective-permute-start(bf16[1024,256]{1,0:T(8,128)(2,1)S(1)} %get-tuple-element.9), channel_id=1, source_target_pairs={{8,0},{16,8},{24,16},{32,24},{40,32},{48,40},{56,48},{64,56},{72,6... | collective-permute-start | bytes 1572872 | tf_op jit(solution)/shard_map/ppermute | solution.py:23
  78.8 6.7 %collective-permute-done.1 = bf16[1024,256]{1,0:T(8,128)(2,1)S(1)} collective-permute-done((bf16[1024,256]{1,0:T(8,128)(2,1)S(1)}, bf16[1024,256]{1,0:T(8,128)(2,1)S(1)}, u32[]{:S(2)}, u32[]{:S(2)}) %collective-permute-start.1) | collective-permute-done | bytes 524320 | tf_op jit(solution)/shard_map/ppermute | solution.py:23
  85.5 0.1 fusion
  85.6 37.8 %all_to_all.10.joined = bf16[8,128,1280]{2,1,0:T(8,128)(2,1)} all-to-all(bf16[8,128,1280]{2,1,0:T(8,128)(2,1)S(1)} %bitcast.6), channel_id=1, replica_groups=mesh['blk'=32,'head'=8] {'head'}, dimensions={0} | all-to-all | bytes 5242880 | tf_op jit(solution)/shard_map/all_to_all | solution.py:171
  123.4 3.5 %unpack.1 = (bf16[128,4096]{1,0:T(8,128)(2,1)}, bf16[128,4096]{1,0:T(8,128)(2,1)}, bf16[128,1024]{1,0:T(8,128)(2,1)}, bf16[128,1024]{1,0:T(8,128)(2,1)}) custom-call(bf16[8,128,1280]{2,1,0:T(8,128)(2,1)} %all_to_all.10.joined), custom_call_target="tpu_custom_call" | custom-call | tf_op jit(solution)/shard_map/unpack/pallas_call | solution.py:160
  (4 shorter events, 0.0 us)
Async XLA Ops:
  4.1 7.0 %copy-start = (s32[64]{0:T(128)S(1)}, s32[64]{0:T(128)}, u32[]{:S(2)}) copy-start(s32[64]{0:T(128)} %param.9) | copy-start | bytes 772
  4.1 45.4 %all-to-all-start = ((bf16[8,128,1280]{2,1,0:T(8,128)(2,1)}), bf16[8,128,1280]{2,1,0:T(8,128)(2,1)S(1)}, u32[]{:S(2)}, u32[]{:S(2)}) async-start(bf16[8,128,1280]{2,1,0:T(8,128)(2,1)} %pack.1), calls=%async_computation | async-start | bytes 5242880 | tf_op jit(solution)/shard_map/all_to_all | solution.py:171
  50.3 11.7 %collective-permute-start = (bf16[1024,256]{1,0:T(8,128)(2,1)}, bf16[1024,256]{1,0:T(8,128)(2,1)}, u32[]{:S(2)}, u32[]{:S(2)}) collective-permute-start(bf16[1024,256]{1,0:T(8,128)(2,1)} %slice.8), channel_id=1, source_target_pairs={{0,8},{8,16},{16,24},{24,32},{32,40},{40,48},{48,56},{56,64},{64,7... | collective-permute-start | bytes 1572872 | tf_op jit(solution)/shard_map/ppermute | solution.py:23
  76.9 8.6 %collective-permute-start.1 = (bf16[1024,256]{1,0:T(8,128)(2,1)S(1)}, bf16[1024,256]{1,0:T(8,128)(2,1)S(1)}, u32[]{:S(2)}, u32[]{:S(2)}) collective-permute-start(bf16[1024,256]{1,0:T(8,128)(2,1)S(1)} %get-tuple-element.9), channel_id=1, source_target_pairs={{8,0},{16,8},{24,16},{32,24},{40,32},{48,40},{56,48},{64,56},{72,6... | collective-permute-start | bytes 1572872 | tf_op jit(solution)/shard_map/ppermute | solution.py:23
where the time goes:
time: 127 us
  waiting for transfers between devices  54.1 us (43%)
  blocking collectives  37.8 us (30%)
  Pallas kernels  21.8 us (17%)
  starting transfers between devices  10.8 us (9%)
    all_to_all x1, waiting for transfers between devices, exchange(): lax.all_to_all(value, 'head', split_axis=0, concat_axis=0, tiled=True)  38.1 us
    all_to_all x1, blocking collectives, exchange(): lax.all_to_all(value, 'head', split_axis=0, concat_axis=0, tiled=True)  37.8 us
    ppermute x2, waiting for transfers between devices, passed_along(): lax.ppermute(value, axis, [(source, source + steps) for source in range(i...  16 us
    pallas_call x1, Pallas kernels, attention(): pl.pallas_call(functools.partial(attention_kernel, heads, block, most, pa...  14.9 us
    all_to_all x1, starting transfers between devices, exchange(): lax.all_to_all(value, 'head', split_axis=0, concat_axis=0, tiled=True)  6.94 us
    ppermute x2, starting transfers between devices, passed_along(): lax.ppermute(value, axis, [(source, source + steps) for source in range(i...  3.83 us
    pallas_call x1, Pallas kernels, unpack(): pl.pallas_call(functools.partial(unpack_kernel, count), in_specs=[pl.Bloc...  3.48 us
    pallas_call x1, Pallas kernels, pack(): pl.pallas_call(functools.partial(pack_kernel, count), in_specs=[pl.BlockS...  3.44 us
  transfers between devices with their start and end apart: 3, of which 3 were waited for; matrix products, arithmetic and copies ran while one was open for 1% of the time, Pallas kernels for 0%

commit v1 on v0

--- a/solution.py
+++ b/solution.py
@@ -138,8 +138,20 @@
 
 
 def unpack_kernel(count, joined, *refs):
-    *wholes, sems = refs
-    moves([(target, source) for source, target in portions(count, wholes, joined)], sems)
+    *wholes, held, arrivals, sems = refs
+    arriving = [pltpu.make_async_copy(joined.at[h], held.at[h], arrivals.at[h]) for h in range(count)]
+    for copy in arriving:
+        copy.start()
+    leaving = portions(count, wholes, held)
+    started = []
+    for h in range(count):
+        arriving[h].wait()
+        for i in range(h, len(leaving), count):
+            target, source = leaving[i]
+            started.append(pltpu.make_async_copy(source, target, sems.at[i]))
+            started[-1].start()
+    for copy in started:
+        copy.wait()
 
 
 def pack(count, *wholes):
@@ -159,10 +171,14 @@
     count, rows, _ = joined.shape
     return pl.pallas_call(
         functools.partial(unpack_kernel, count),
-        in_specs=[pl.BlockSpec(memory_space=pltpu.VMEM)],
+        in_specs=[pl.BlockSpec(memory_space=pl.ANY)],
         out_specs=[pl.BlockSpec(memory_space=pl.ANY)] * len(widths),
         out_shape=[jax.ShapeDtypeStruct((rows, count * width), joined.dtype) for width in widths],
-        scratch_shapes=[pltpu.SemaphoreType.DMA((len(widths) * count,))],
+        scratch_shapes=[
+            pltpu.VMEM(joined.shape, joined.dtype),
+            pltpu.SemaphoreType.DMA((count,)),
+            pltpu.SemaphoreType.DMA((len(widths) * count,)),
+        ],
         name="unpack",
     )(joined)
 
@@ -178,15 +194,15 @@
     pair = 2 * HEAD_DIM
     middle = query.shape[1] // count
 
+    packed = pack(count, query, grad_out, key, value)
+    packed, place = lax.optimization_barrier((packed, lax.axis_index("blk")))
+    entered, doc_lengths, place = lax.optimization_barrier((exchange(packed).reshape(block, -1), doc_lengths, place))
     doc_ends = jnp.cumsum(doc_lengths)
     doc_starts = doc_ends - doc_lengths
-    origin = lax.axis_index("blk") * block - block
+    origin = place * block - block
     positions = origin + block + jnp.arange(block, dtype=jnp.int32)
     starts = jnp.max(jnp.where(doc_starts[None, :] <= positions[:, None], doc_starts[None, :], 0), axis=1)
     starts = (starts - origin).astype(jnp.int32)
-
-    packed = pack(count, query, grad_out, key, value)
-    entered = exchange(packed).reshape(block, -1)
     earlier = passed_along(entered[:, 2 * middle :], "blk", 1)
     out, earlier_sums, own_sums = attention(entered, earlier, starts)
     returned = passed_along(earlier_sums, "blk", -1)

time: 127 us -> 122 us (0.961); the launches traced: 127 us -> 121 us
  blocking collectives: 37.8 us -> 78 us
  waiting for transfers between devices: 54.1 us -> 16 us
  starting transfers between devices: 10.8 us -> 5.97 us
  Pallas kernels: 21.8 us -> 18.2 us
    all_to_all x1 -> x2, blocking collectives: 37.8 us -> 78 us  [exchange(): lax.all_to_all(value, 'head', split_axis=0, concat_axis=0, tiled=True)]
    all_to_all x1 -> x0, waiting for transfers between devices: 38.1 us -> none  [exchange(): lax.all_to_all(value, 'head', split_axis=0, concat_axis=0, tiled=True)]
    all_to_all x1 -> x0, starting transfers between devices: 6.94 us -> none  [exchange(): lax.all_to_all(value, 'head', split_axis=0, concat_axis=0, tiled=True)]
    pallas_call x1, Pallas kernels: 14.9 us -> 12 us  [attention(): pl.pallas_call(functools.partial(attention_kernel, heads, block, most, pa...]
    ppermute x2, starting transfers between devices: 3.83 us -> 5.97 us  [passed_along(): lax.ppermute(value, axis, [(source, source + steps) for source in range(i...]
  transfers between devices with their start and end apart: 3 -> 2, of which waited for: 3 -> 2; matrix products, arithmetic and copies ran while one was open for 1% -> 0% of each run, Pallas kernels for 0% -> 0%
where the time goes in v1:
time: 122 us; the launch traced here: 121 us
  blocking collectives  78 us (64%)
  Pallas kernels  18.2 us (15%)
  waiting for transfers between devices  16 us (13%)
  starting transfers between devices  5.97 us (5%)
  local copies, waits for them, and re-layouts  1.25 us (1%)
    all_to_all x2, blocking collectives, exchange(): lax.all_to_all(value, 'head', split_axis=0, concat_axis=0, tiled=True)  78 us
    ppermute x2, waiting for transfers between devices, passed_along(): lax.ppermute(value, axis, [(source, source + steps) for source in range(i...  16 us
    pallas_call x1, Pallas kernels, attention(): pl.pallas_call(functools.partial(attention_kernel, heads, block, most, pa...  12 us
    ppermute x2, starting transfers between devices, passed_along(): lax.ppermute(value, axis, [(source, source + steps) for source in range(i...  5.97 us
    pallas_call x1, Pallas kernels, pack(): pl.pallas_call(functools.partial(pack_kernel, count), in_specs=[pl.BlockS...  3.44 us
    pallas_call x1, Pallas kernels, unpack(): pl.pallas_call(functools.partial(unpack_kernel, count), in_specs=[pl.Bloc...  2.78 us
  transfers between devices with their start and end apart: 2, of which 2 were waited for; matrix products, arithmetic and copies ran while one was open for 0% of the time, Pallas kernels for 0%

profile of v1, /device:TPU:192, one launch (start us, length us, event | category | flops | bytes accessed | tf_op | source)
XLA Modules:
  0.0 120.5 jit_solution(9271614882490382120)
XLA Ops:
  0.6 3.4 %pack.1 = bf16[8,128,1280]{2,1,0:T(8,128)(2,1)} custom-call(bf16[128,4096]{1,0:T(8,128)(2,1)} %refs_0_.1, bf16[128,4096]{1,0:T(8,128)(2,1)} %refs_1_.1, bf16[128,1024]{1,0:T(8,128)(2,1)} %refs_2_.1, bf16[128,1024]{1,0:T(8,128)(2,1)} %refs_3_.1), custom_call_target="tpu_custom_call" | custom-call | tf_op jit(solution)/shard_map/pack/pallas_call | solution.py:160
  4.1 0.0 copy-start
  4.1 40.6 %all_to_all.10 = bf16[8,128,1280]{2,1,0:T(8,128)(2,1)S(1)} all-to-all(bf16[8,128,1280]{2,1,0:T(8,128)(2,1)} %pack.1), channel_id=1, replica_groups=mesh['blk'=32,'head'=8] {'head'}, dimensions={0} | all-to-all | bytes 5242880 | tf_op jit(solution)/shard_map/all_to_all | solution.py:187
  44.7 0.0 copy-done
  44.7 0.1 copy.12
  44.8 0.1 reduce-window.9
  44.9 0.1 reduce
  45.1 0.8 slice.7
  45.9 1.9 %collective-permute-start = (bf16[1024,256]{1,0:T(8,128)(2,1)}, bf16[1024,256]{1,0:T(8,128)(2,1)}, u32[]{:S(2)}, u32[]{:S(2)}) collective-permute-start(bf16[1024,256]{1,0:T(8,128)(2,1)} %slice.7), channel_id=1, source_target_pairs={{0,8},{8,16},{16,24},{24,32},{32,40},{40,48},{48,56},{56,64},{64,7... | collective-permute-start | bytes 1572872 | tf_op jit(solution)/shard_map/ppermute | solution.py:23
  47.8 0.1 select_reduce_fusion
  47.9 0.1 slice.6
  48.0 0.2 copy.13.start_ref
  48.3 9.3 %collective-permute-done.earlier_ref = bf16[1024,256]{1,0:T(8,128)(2,1)} collective-permute-done((bf16[1024,256]{1,0:T(8,128)(2,1)}, bf16[1024,256]{1,0:T(8,128)(2,1)}, u32[]{:S(2)}, u32[]{:S(2)}) %collective-permute-start) | collective-permute-done | bytes 524320 | tf_op jit(solution)/shard_map/ppermute | solution.py:23
  57.6 12.0 %attention.1 = (bf16[1024,1280]{1,0:T(8,128)(2,1)S(1)}, bf16[1024,256]{1,0:T(8,128)(2,1)S(1)}, f32[1024,256]{1,0:T(8,128)S(1)}) custom-call(s32[8]{0:T(128)S(1)} %fusion.1.counts_ref, s32[1024,1]{1,0:T(8,128)S(1)} %copy.13.start_ref, bf16[1024,1280]{1,0:T(8,128)(2,1)S(1)} %bitcast.5, bf16[1024,256]{1,0:T(8,128)(2,1)} %collective-permute-done.earlier_ref), custom_call_target="tpu_custom_call" | custom-call | flops 6442450944 | bytes 5242880 | tf_op jit(solution)/shard_map/attention/pallas_call | solution.py:96
  69.6 4.1 %collective-permute-start.1 = (bf16[1024,256]{1,0:T(8,128)(2,1)S(1)}, bf16[1024,256]{1,0:T(8,128)(2,1)S(1)}, u32[]{:S(2)}, u32[]{:S(2)}) collective-permute-start(bf16[1024,256]{1,0:T(8,128)(2,1)S(1)} %get-tuple-element.19), channel_id=1, source_target_pairs={{8,0},{16,8},{24,16},{32,24},{40,32},{48,40},{56,48},{64,56},{72,6... | collective-permute-start | bytes 1572872 | tf_op jit(solution)/shard_map/ppermute | solution.py:23
  73.6 6.7 %collective-permute-done.1 = bf16[1024,256]{1,0:T(8,128)(2,1)S(1)} collective-permute-done((bf16[1024,256]{1,0:T(8,128)(2,1)S(1)}, bf16[1024,256]{1,0:T(8,128)(2,1)S(1)}, u32[]{:S(2)}, u32[]{:S(2)}) %collective-permute-start.1) | collective-permute-done | bytes 524320 | tf_op jit(solution)/shard_map/ppermute | solution.py:23
  80.3 0.1 fusion
  80.4 37.3 %all_to_all.11.joined = bf16[8,128,1280]{2,1,0:T(8,128)(2,1)} all-to-all(bf16[8,128,1280]{2,1,0:T(8,128)(2,1)S(1)} %bitcast.6), channel_id=1, replica_groups=mesh['blk'=32,'head'=8] {'head'}, dimensions={0} | all-to-all | bytes 5242880 | tf_op jit(solution)/shard_map/all_to_all | solution.py:187
  117.8 2.8 %unpack.1 = (bf16[128,4096]{1,0:T(8,128)(2,1)}, bf16[128,4096]{1,0:T(8,128)(2,1)}, bf16[128,1024]{1,0:T(8,128)(2,1)}, bf16[128,1024]{1,0:T(8,128)(2,1)}) custom-call(bf16[8,128,1280]{2,1,0:T(8,128)(2,1)} %all_to_all.11.joined), custom_call_target="tpu_custom_call" | custom-call | tf_op jit(solution)/shard_map/unpack/pallas_call | solution.py:172
  (4 shorter events, 0.0 us)
Async XLA Ops:
  4.1 40.7 %copy-start = (s32[64]{0:T(128)S(1)}, s32[64]{0:T(128)}, u32[]{:S(2)}) copy-start(s32[64]{0:T(128)} %param.9) | copy-start | bytes 772
  45.9 11.7 %collective-permute-start = (bf16[1024,256]{1,0:T(8,128)(2,1)}, bf16[1024,256]{1,0:T(8,128)(2,1)}, u32[]{:S(2)}, u32[]{:S(2)}) collective-permute-start(bf16[1024,256]{1,0:T(8,128)(2,1)} %slice.7), channel_id=1, source_target_pairs={{0,8},{8,16},{16,24},{24,32},{32,40},{40,48},{48,56},{56,64},{64,7... | collective-permute-start | bytes 1572872 | tf_op jit(solution)/shard_map/ppermute | solution.py:23
  69.6 10.7 %collective-permute-start.1 = (bf16[1024,256]{1,0:T(8,128)(2,1)S(1)}, bf16[1024,256]{1,0:T(8,128)(2,1)S(1)}, u32[]{:S(2)}, u32[]{:S(2)}) collective-permute-start(bf16[1024,256]{1,0:T(8,128)(2,1)S(1)} %get-tuple-element.19), channel_id=1, source_target_pairs={{8,0},{16,8},{24,16},{32,24},{40,32},{48,40},{56,48},{64,56},{72,6... | collective-permute-start | bytes 1572872 | tf_op jit(solution)/shard_map/ppermute | solution.py:23
